TPU v7x, 512 devices: a whole 4x8x8 slice. The times are simulated.
512 devices in a mesh: row: 32 (over z_hi, y, core), col: 16 (over z_lo, x).
Axes of the slice: x: 4, y: 8, z: 8 (z_hi: 2, z_lo: 4; z = z_hi * 4 + z_lo), core: 2. Of those that a mesh axis runs over, the one named last changes fastest.
Arguments:
- sources: float32 [32, 16, 512, 512], P('row', 'col'), may hold values from -6 to 6
- leaf_basis: float32 [32, 16, 512, 256], P('row', 'col'), may hold values from -0.25 to 0.25
- transfers: float32 [32, 16, 4, 256, 512], P('row', 'col'), may hold values from -0.25 to 0.25
- out_basis: float32 [32, 16, 512, 256], P('row', 'col'), may hold values from -0.375 to 0.375
Outputs:
- result: float32 [32, 16, 512, 512], P('row', 'col')
All inputs are finite; a program needn't handle non-finite values.
Results may differ from a plain program's by a relative error of at most 0.0001.
Values sent between devices are 32-bit elements; how exact they have to be, the bound alone decides.
No kernel may reach another device: no remote copies, remote signals or barrier semaphores. Data moves between devices by JAX's collectives and lax.ppermute only.
A program may use at most 64 MiB of HBM per device.

v0:
```python
import jax
import jax.numpy as jnp
from jax import lax
from jax.sharding import PartitionSpec as P


def swapped(x, axis, apart):
    return lax.ppermute(x, axis, [(i, i ^ 1 << apart) for i in range(lax.axis_size(axis))])


def mix_level(block, coeff, other):
    high = lax.Precision.HIGHEST
    width = coeff.shape[0]
    own = jnp.dot(block[:, :width], coeff, precision=high, preferred_element_type=jnp.float32)
    return own + jnp.dot(
        block[:, width:], other, precision=high, preferred_element_type=jnp.float32
    )


def body(sources, leaf_basis, transfers, out_basis):
    high = lax.Precision.HIGHEST
    levels = transfers.shape[2]
    row_bits = lax.axis_size("row").bit_length() - 1
    col_bits = lax.axis_size("col").bit_length() - 1
    coeff = jnp.einsum("mk,mr->kr", leaf_basis[0, 0], sources[0, 0], precision=high)
    half = coeff.shape[1] // 2
    groups = [coeff[:, :half], coeff[:, half:]]
    for level in range(levels):
        fresh = []
        for member in groups:
            if level % 2 == 0:
                other = swapped(member, "row", row_bits - 1 - level // 2)
            else:
                other = swapped(member, "col", col_bits - 1 - level // 2)
            fresh.append(mix_level(transfers[0, 0, level], member, other))
        groups = fresh
    coeff = jnp.concatenate(groups, axis=1)
    result = jnp.dot(out_basis[0, 0], coeff, precision=high, preferred_element_type=jnp.float32)
    return result[None, None]


def solution(mesh):
    in_specs = (
        P("row", "col", None, None),
        P("row", "col", None, None),
        P("row", "col", None, None, None),
        P("row", "col", None, None),
    )
    out_specs = P("row", "col", None, None)
    return jax.shard_map(body, mesh=mesh, in_specs=in_specs, out_specs=out_specs, check_vma=False)
```

profile of v0, /device:TPU:16, one launch (start us, length us, event | category | flops | bytes accessed | tf_op | source)
XLA Modules:
  0.0 104.7 jit_solution(4719273634697918270)
XLA Ops:
  0.0 1.2 %copy-done = f32[1,1,512,512]{3,2,1,0:T(8,128)S(1)} copy-done((f32[1,1,512,512]{3,2,1,0:T(8,128)S(1)}, f32[1,1,512,512]{3,2,1,0:T(8,128)}, u32[]{:S(2)}) %copy-start) | copy-done | bytes 1048600
  1.2 2.1 %fusion.2 = f32[256,512]{1,0:T(8,128)S(1)} fusion(f32[1,1,512,512]{3,2,1,0:T(8,128)S(1)} %copy-done, f32[1,1,512,256]{3,2,1,0:T(8,128)} %param.5), kind=kOutput, calls=%fused_computation.11 | convolution fusion | flops 805306368 | bytes 2097152 | tf_op jit(solution)/shard_map/mk,mr->kr/dot_general | solution.py:25
  3.4 10.9 %collective-permute-start = (f32[256,256]{1,0:T(8,128)S(1)}, f32[256,256]{1,0:T(8,128)S(1)}, u32[]{:S(2)}, u32[]{:S(2)}) collective-permute-start(f32[256,256]{1,0:T(8,128)S(1)} %get-tuple-element.9), channel_id=1, source_target_pairs={{0,256},{16,272},{32,288},{48,304},{64,320},{80,336},{96,352},{112... | collective-permute-start | bytes 786440 | tf_op jit(solution)/shard_map/ppermute | solution.py:8
  14.3 1.9 %collective-permute-start.4 = (f32[256,256]{1,0:T(8,128)S(1)}, f32[256,256]{1,0:T(8,128)S(1)}, u32[]{:S(2)}, u32[]{:S(2)}) collective-permute-start(f32[256,256]{1,0:T(8,128)S(1)} %get-tuple-element.10), channel_id=1, source_target_pairs={{0,256},{16,272},{32,288},{48,304},{64,320},{80,336},{96,352},{112... | collective-permute-start | bytes 786440 | tf_op jit(solution)/shard_map/ppermute | solution.py:8
  16.4 0.6 fusion.29
  17.0 0.6 fusion.31
  17.6 11.9 %collective-permute-done.4 = f32[256,256]{1,0:T(8,128)S(1)} collective-permute-done((f32[256,256]{1,0:T(8,128)S(1)}, f32[256,256]{1,0:T(8,128)S(1)}, u32[]{:S(2)}, u32[]{:S(2)}) %collective-permute-start.4) | collective-permute-done | bytes 262176 | tf_op jit(solution)/shard_map/ppermute | solution.py:8
  29.6 0.6 convolution_add_fusion.3
  30.2 12.3 %collective-permute-start.5 = (f32[256,256]{0,1:T(8,128)S(1)}, f32[256,256]{0,1:T(8,128)S(1)}, u32[]{:S(2)}, u32[]{:S(2)}) collective-permute-start(f32[256,256]{0,1:T(8,128)S(1)} %bitcast.46), channel_id=1, source_target_pairs={{0,8},{1,9},{2,10},{3,11},{4,12},{5,13},{6,14},{7,15},{8,0},{9,1},... | collective-permute-start | bytes 786440 | tf_op jit(solution)/shard_map/ppermute | solution.py:8
  42.5 0.6 convolution_add_fusion.7
  43.1 0.4 fusion.25
  43.5 1.9 %collective-permute-start.1 = (f32[256,256]{0,1:T(8,128)S(1)}, f32[256,256]{0,1:T(8,128)S(1)}, u32[]{:S(2)}, u32[]{:S(2)}) collective-permute-start(f32[256,256]{0,1:T(8,128)S(1)} %bitcast.47), channel_id=1, source_target_pairs={{0,8},{1,9},{2,10},{3,11},{4,12},{5,13},{6,14},{7,15},{8,0},{9,1},... | collective-permute-start | bytes 786440 | tf_op jit(solution)/shard_map/ppermute | solution.py:8
  45.4 0.4 fusion.23
  45.9 14.7 %collective-permute-done.5 = f32[256,256]{0,1:T(8,128)S(1)} collective-permute-done((f32[256,256]{0,1:T(8,128)S(1)}, f32[256,256]{0,1:T(8,128)S(1)}, u32[]{:S(2)}, u32[]{:S(2)}) %collective-permute-start.5) | collective-permute-done | bytes 262176 | tf_op jit(solution)/shard_map/ppermute | solution.py:8
  60.5 0.4 convolution_add_fusion.2
  61.0 5.9 %collective-permute-start.6 = (f32[256,256]{0,1:T(8,128)S(1)}, f32[256,256]{0,1:T(8,128)S(1)}, u32[]{:S(2)}, u32[]{:S(2)}) collective-permute-start(f32[256,256]{0,1:T(8,128)S(1)} %bitcast.48), channel_id=1, source_target_pairs={{0,128},{16,144},{32,160},{48,176},{64,192},{80,208},{96,224},{112... | collective-permute-start | bytes 786440 | tf_op jit(solution)/shard_map/ppermute | solution.py:8
  66.9 0.4 convolution_add_fusion.6
  67.4 0.4 fusion.17
  67.8 4.7 %collective-permute-start.2 = (f32[256,256]{0,1:T(8,128)S(1)}, f32[256,256]{0,1:T(8,128)S(1)}, u32[]{:S(2)}, u32[]{:S(2)}) collective-permute-start(f32[256,256]{0,1:T(8,128)S(1)} %bitcast.49), channel_id=1, source_target_pairs={{0,128},{16,144},{32,160},{48,176},{64,192},{80,208},{96,224},{112... | collective-permute-start | bytes 786440 | tf_op jit(solution)/shard_map/ppermute | solution.py:8
  72.4 0.4 fusion.19
  72.9 10.3 %collective-permute-done.6 = f32[256,256]{0,1:T(8,128)S(1)} collective-permute-done((f32[256,256]{0,1:T(8,128)S(1)}, f32[256,256]{0,1:T(8,128)S(1)}, u32[]{:S(2)}, u32[]{:S(2)}) %collective-permute-start.6) | collective-permute-done | bytes 262176 | tf_op jit(solution)/shard_map/ppermute | solution.py:8
  83.2 0.4 convolution_add_fusion.1
  83.6 1.9 %collective-permute-start.7 = (f32[256,256]{0,1:T(8,128)S(1)}, f32[256,256]{0,1:T(8,128)S(1)}, u32[]{:S(2)}, u32[]{:S(2)}) collective-permute-start(f32[256,256]{0,1:T(8,128)S(1)} %bitcast.45), channel_id=1, source_target_pairs={{0,4},{1,5},{2,6},{3,7},{4,0},{5,1},{6,2},{7,3},{8,12},{9,13},{10,... | collective-permute-start | bytes 786440 | tf_op jit(solution)/shard_map/ppermute | solution.py:8
  85.5 5.5 %collective-permute-done.2 = f32[256,256]{0,1:T(8,128)S(1)} collective-permute-done((f32[256,256]{0,1:T(8,128)S(1)}, f32[256,256]{0,1:T(8,128)S(1)}, u32[]{:S(2)}, u32[]{:S(2)}) %collective-permute-start.2) | collective-permute-done | bytes 262176 | tf_op jit(solution)/shard_map/ppermute | solution.py:8
  91.0 0.4 convolution_add_fusion.5
  91.8 1.9 %collective-permute-start.3 = (f32[256,256]{0,1:T(8,128)S(1)}, f32[256,256]{0,1:T(8,128)S(1)}, u32[]{:S(2)}, u32[]{:S(2)}) collective-permute-start(f32[256,256]{0,1:T(8,128)S(1)} %bitcast.50), channel_id=1, source_target_pairs={{0,4},{1,5},{2,6},{3,7},{4,0},{5,1},{6,2},{7,3},{8,12},{9,13},{10,... | collective-permute-start | bytes 786440 | tf_op jit(solution)/shard_map/ppermute | solution.py:8
  93.7 0.4 fusion.13
  94.2 0.4 fusion
  94.6 7.3 %collective-permute-done.3 = f32[256,256]{0,1:T(8,128)S(1)} collective-permute-done((f32[256,256]{0,1:T(8,128)S(1)}, f32[256,256]{0,1:T(8,128)S(1)}, u32[]{:S(2)}, u32[]{:S(2)}) %collective-permute-start.3) | collective-permute-done | bytes 262176 | tf_op jit(solution)/shard_map/ppermute | solution.py:8
  101.9 0.4 fusion.1
  102.3 1.0 convolution_bitcast_fusion
  103.4 1.3 %copy.5 = f32[1,1,512,512]{3,2,1,0:T(8,128)} copy(f32[1,1,512,512]{2,3,1,0:T(8,128)S(1)} %convolution_bitcast_fusion) | data formatting | bytes 2097152 | tf_op jit(solution)/shard_map/broadcast_in_dim | solution.py:39
  (11 shorter events, 0.6 us)
Async XLA Ops:
  0.0 1.2 %copy-start = (f32[1,1,512,512]{3,2,1,0:T(8,128)S(1)}, f32[1,1,512,512]{3,2,1,0:T(8,128)}, u32[]{:S(2)}) copy-start(f32[1,1,512,512]{3,2,1,0:T(8,128)} %param.4) | copy-start | bytes 3145732
  0.0 16.2 %copy-start.1 = (f32[1,1,4,256,512]{4,3,2,1,0:T(8,128)S(1)}, f32[1,1,4,256,512]{4,3,2,1,0:T(8,128)}, u32[]{:S(2)}) copy-start(f32[1,1,4,256,512]{4,3,2,1,0:T(8,128)} %param.6) | copy-start | bytes 6291460
  3.4 39.1 %collective-permute-start = (f32[256,256]{1,0:T(8,128)S(1)}, f32[256,256]{1,0:T(8,128)S(1)}, u32[]{:S(2)}, u32[]{:S(2)}) collective-permute-start(f32[256,256]{1,0:T(8,128)S(1)} %get-tuple-element.9), channel_id=1, source_target_pairs={{0,256},{16,272},{32,288},{48,304},{64,320},{80,336},{96,352},{112... | collective-permute-start | bytes 786440 | tf_op jit(solution)/shard_map/ppermute | solution.py:8
  14.3 15.2 %collective-permute-start.4 = (f32[256,256]{1,0:T(8,128)S(1)}, f32[256,256]{1,0:T(8,128)S(1)}, u32[]{:S(2)}, u32[]{:S(2)}) collective-permute-start(f32[256,256]{1,0:T(8,128)S(1)} %get-tuple-element.10), channel_id=1, source_target_pairs={{0,256},{16,272},{32,288},{48,304},{64,320},{80,336},{96,352},{112... | collective-permute-start | bytes 786440 | tf_op jit(solution)/shard_map/ppermute | solution.py:8
  30.2 30.4 %collective-permute-start.5 = (f32[256,256]{0,1:T(8,128)S(1)}, f32[256,256]{0,1:T(8,128)S(1)}, u32[]{:S(2)}, u32[]{:S(2)}) collective-permute-start(f32[256,256]{0,1:T(8,128)S(1)} %bitcast.46), channel_id=1, source_target_pairs={{0,8},{1,9},{2,10},{3,11},{4,12},{5,13},{6,14},{7,15},{8,0},{9,1},... | collective-permute-start | bytes 786440 | tf_op jit(solution)/shard_map/ppermute | solution.py:8
  43.5 23.4 %collective-permute-start.1 = (f32[256,256]{0,1:T(8,128)S(1)}, f32[256,256]{0,1:T(8,128)S(1)}, u32[]{:S(2)}, u32[]{:S(2)}) collective-permute-start(f32[256,256]{0,1:T(8,128)S(1)} %bitcast.47), channel_id=1, source_target_pairs={{0,8},{1,9},{2,10},{3,11},{4,12},{5,13},{6,14},{7,15},{8,0},{9,1},... | collective-permute-start | bytes 786440 | tf_op jit(solution)/shard_map/ppermute | solution.py:8
  61.0 22.2 %collective-permute-start.6 = (f32[256,256]{0,1:T(8,128)S(1)}, f32[256,256]{0,1:T(8,128)S(1)}, u32[]{:S(2)}, u32[]{:S(2)}) collective-permute-start(f32[256,256]{0,1:T(8,128)S(1)} %bitcast.48), channel_id=1, source_target_pairs={{0,128},{16,144},{32,160},{48,176},{64,192},{80,208},{96,224},{112... | collective-permute-start | bytes 786440 | tf_op jit(solution)/shard_map/ppermute | solution.py:8
  67.8 23.2 %collective-permute-start.2 = (f32[256,256]{0,1:T(8,128)S(1)}, f32[256,256]{0,1:T(8,128)S(1)}, u32[]{:S(2)}, u32[]{:S(2)}) collective-permute-start(f32[256,256]{0,1:T(8,128)S(1)} %bitcast.49), channel_id=1, source_target_pairs={{0,128},{16,144},{32,160},{48,176},{64,192},{80,208},{96,224},{112... | collective-permute-start | bytes 786440 | tf_op jit(solution)/shard_map/ppermute | solution.py:8
  83.6 10.6 %collective-permute-start.7 = (f32[256,256]{0,1:T(8,128)S(1)}, f32[256,256]{0,1:T(8,128)S(1)}, u32[]{:S(2)}, u32[]{:S(2)}) collective-permute-start(f32[256,256]{0,1:T(8,128)S(1)} %bitcast.45), channel_id=1, source_target_pairs={{0,4},{1,5},{2,6},{3,7},{4,0},{5,1},{6,2},{7,3},{8,12},{9,13},{10,... | collective-permute-start | bytes 786440 | tf_op jit(solution)/shard_map/ppermute | solution.py:8
  91.4 10.9 %copy-start.2 = (f32[1,1,512,256]{3,2,1,0:T(8,128)S(1)}, f32[1,1,512,256]{3,2,1,0:T(8,128)}, u32[]{:S(2)}) copy-start(f32[1,1,512,256]{3,2,1,0:T(8,128)} %param.7) | copy-start | bytes 1572868
  91.8 10.1 %collective-permute-start.3 = (f32[256,256]{0,1:T(8,128)S(1)}, f32[256,256]{0,1:T(8,128)S(1)}, u32[]{:S(2)}, u32[]{:S(2)}) collective-permute-start(f32[256,256]{0,1:T(8,128)S(1)} %bitcast.50), channel_id=1, source_target_pairs={{0,4},{1,5},{2,6},{3,7},{4,0},{5,1},{6,2},{7,3},{8,12},{9,13},{10,... | collective-permute-start | bytes 786440 | tf_op jit(solution)/shard_map/ppermute | solution.py:8
where the time goes:
time: 105 us
  waiting for transfers between devices  49.7 us (47%)
  starting transfers between devices  41.5 us (40%)
  matrix products  10.5 us (10%)
  local copies, waits for them, and re-layouts  2.75 us (3%)
    ppermute x8, waiting for transfers between devices, swapped(): lax.ppermute(x, axis, [(i, i ^ 1 << apart) for i in range(lax.axis_size(a...  49.7 us
    ppermute x8, starting transfers between devices, swapped(): lax.ppermute(x, axis, [(i, i ^ 1 << apart) for i in range(lax.axis_size(a...  41.5 us
    dot_general x8, matrix products, mix_level(): jnp.dot(block[:, width:], other, precision=high, preferred_element_type=j...  3.67 us
    dot_general x8, matrix products, mix_level(): jnp.dot(block[:, :width], coeff, precision=high, preferred_element_type=j...  3.65 us
  transfers between devices with their start and end apart: 8, of which 5 were waited for; matrix products, arithmetic and copies ran while one was open for 7% of the time, Pallas kernels for 0%

commit v1 on v0

v1 whole, which is shorter than its diff:
```python
import jax
import jax.numpy as jnp
from jax import lax
from jax.experimental.layout import Layout, with_layout_constraint
from jax.sharding import PartitionSpec as P

STEPS = [(0, 0, 1), (0, 1, 2), (0, 2, 3), (0, 3, 4), (1, 0, 1), (1, 1, 2), (1, 2, 3), (1, 3, 4), (2, 0, 1), (2, 1, 2), (2, 2, 3), (2, 3, 4), (3, 0, 1), (3, 1, 2), (3, 2, 3), (3, 3, 4), (4, 0, 1), (4, 1, 2), (4, 2, 3), (4, 3, 4)]
PARTS = 4
HIGH = lax.Precision.HIGH


def swapped(x, axis, apart):
    return lax.ppermute(x, axis, [(i, i ^ 1 << apart) for i in range(lax.axis_size(axis))])


def dot(a, b):
    return jnp.dot(a, b, precision=HIGH, preferred_element_type=jnp.float32)


def pinned(x):
    return with_layout_constraint(x, Layout((0, 1)))


def body(sources, leaf_basis, transfers, out_basis):
    levels = transfers.shape[2]
    rank, width = leaf_basis.shape[3], sources.shape[3] // PARTS
    row_bits = lax.axis_size("row").bit_length() - 1
    col_bits = lax.axis_size("col").bit_length() - 1

    def partner(x, level):
        if level % 2 == 0:
            return swapped(x, "row", row_bits - 1 - level // 2)
        return swapped(x, "col", col_bits - 1 - level // 2)

    coeff = jnp.einsum("mk,mr->kr", leaf_basis[0, 0], sources[0, 0], precision=HIGH, preferred_element_type=jnp.float32)
    sent = [[] for _ in range(levels)]
    out, token = [], None
    for level, lo, hi in STEPS:
        if level == 0:
            now = coeff[:, lo * width:hi * width]
            if token is not None:
                now, token = lax.optimization_barrier((now, token))
        else:
            pieces = []
            for a, b, own, other in sent[level - 1]:
                x, y = max(a, lo), min(b, hi)
                if x < y:
                    cut = slice((x - a) * width, (y - a) * width)
                    kept, token = lax.optimization_barrier((own[:, cut], token))
                    pieces.append(kept + dot(transfers[0, 0, level - 1][:, rank:], other[:, cut]))
            now = pinned(jnp.concatenate(pieces, axis=1) if len(pieces) > 1 else pieces[0])
        if level < levels:
            own = dot(transfers[0, 0, level][:, :rank], now)
            sent[level].append((lo, hi, own, partner(now, level)))
            token = own
        else:
            token = pinned(dot(out_basis[0, 0], now))
            out.append((lo, token))
    out = [x for _, x in sorted(out, key=lambda e: e[0])]
    result = jnp.concatenate(out, axis=1) if len(out) > 1 else out[0]
    return result[None, None]


def solution(mesh):
    in_specs = (
        P("row", "col", None, None),
        P("row", "col", None, None),
        P("row", "col", None, None, None),
        P("row", "col", None, None),
    )
    out_specs = P("row", "col", None, None)
    return jax.shard_map(body, mesh=mesh, in_specs=in_specs, out_specs=out_specs, check_vma=False)
```

time: 105 us -> 95.2 us (0.907)
  the two profiles are of different devices: /device:TPU:16 before, /device:TPU:18 now
where the time goes in v1:
time: 95.2 us; the launch traced here: 94.7 us
  starting transfers between devices  63.4 us (67%)
  waiting for transfers between devices  16.1 us (17%)
  matrix products  12.2 us (13%)
  local copies, waits for them, and re-layouts  1.44 us (2%)
  other arithmetic  1.04 us (1%)
    ppermute x16, starting transfers between devices, swapped(): lax.ppermute(x, axis, [(i, i ^ 1 << apart) for i in range(lax.axis_size(a...  63.4 us
    ppermute x16, waiting for transfers between devices, swapped(): lax.ppermute(x, axis, [(i, i ^ 1 << apart) for i in range(lax.axis_size(a...  16.1 us
    dot_general x36, matrix products, dot(): return jnp.dot(a, b, precision=HIGH, preferred_element_type=jnp.float32)  10.5 us
  transfers between devices with their start and end apart: 16, of which 5 were waited for; matrix products, arithmetic and copies ran while one was open for 11% of the time, Pallas kernels for 0%

profile of v1, /device:TPU:18, one launch (start us, length us, event | category | flops | bytes accessed | tf_op | source)
XLA Modules:
  0.0 94.7 jit_solution(2062328247393399481)
XLA Ops:
  0.0 1.2 %copy-done = f32[1,1,512,512]{3,2,1,0:T(8,128)S(1)} copy-done((f32[1,1,512,512]{3,2,1,0:T(8,128)S(1)}, f32[1,1,512,512]{3,2,1,0:T(8,128)}, u32[]{:S(2)}) %copy-start) | copy-done | bytes 1048600
  1.2 1.7 %fusion.16 = f32[256,512]{1,0:T(8,128)S(1)} fusion(f32[1,1,512,512]{3,2,1,0:T(8,128)S(1)} %copy-done, f32[1,1,512,256]{3,2,1,0:T(8,128)} %param.5), kind=kOutput, calls=%fused_computation.53 | convolution fusion | flops 402653184 | bytes 2097152 | tf_op jit(solution)/shard_map/mk,mr->kr/dot_general | solution.py:35
  2.9 10.9 %collective-permute-start = (f32[256,128]{1,0:T(8,128)S(1)}, f32[256,128]{1,0:T(8,128)S(1)}, u32[]{:S(2)}, u32[]{:S(2)}) collective-permute-start(f32[256,128]{1,0:T(8,128)S(1)} %get-tuple-element.47), channel_id=1, source_target_pairs={{0,256},{16,272},{32,288},{48,304},{64,320},{80,336},{96,352},{112... | collective-permute-start | bytes 393224 | tf_op jit(solution)/shard_map/ppermute | solution.py:13
  14.3 1.9 %collective-permute-start.1 = (f32[256,128]{1,0:T(8,128)S(1)}, f32[256,128]{1,0:T(8,128)S(1)}, u32[]{:S(2)}, u32[]{:S(2)}) collective-permute-start(f32[256,128]{1,0:T(8,128)S(1)} %get-tuple-element.24), channel_id=1, source_target_pairs={{0,256},{16,272},{32,288},{48,304},{64,320},{80,336},{96,352},{112... | collective-permute-start | bytes 393224 | tf_op jit(solution)/shard_map/ppermute | solution.py:13
  16.6 7.8 %collective-permute-start.2 = (f32[256,128]{1,0:T(8,128)S(1)}, f32[256,128]{1,0:T(8,128)S(1)}, u32[]{:S(2)}, u32[]{:S(2)}) collective-permute-start(f32[256,128]{1,0:T(8,128)S(1)} %get-tuple-element.25), channel_id=1, source_target_pairs={{0,256},{16,272},{32,288},{48,304},{64,320},{80,336},{96,352},{112... | collective-permute-start | bytes 393224 | tf_op jit(solution)/shard_map/ppermute | solution.py:13
  24.7 1.9 %collective-permute-start.3 = (f32[256,128]{1,0:T(8,128)S(1)}, f32[256,128]{1,0:T(8,128)S(1)}, u32[]{:S(2)}, u32[]{:S(2)}) collective-permute-start(f32[256,128]{1,0:T(8,128)S(1)} %get-tuple-element.26), channel_id=1, source_target_pairs={{0,256},{16,272},{32,288},{48,304},{64,320},{80,336},{96,352},{112... | collective-permute-start | bytes 393224 | tf_op jit(solution)/shard_map/ppermute | solution.py:13
  27.2 4.3 %collective-permute-start.4 = (f32[256,128]{1,0:T(8,128)S(1)}, f32[256,128]{1,0:T(8,128)S(1)}, u32[]{:S(2)}, u32[]{:S(2)}) collective-permute-start(f32[256,128]{1,0:T(8,128)S(1)} %fusion.15), channel_id=1, source_target_pairs={{0,8},{1,9},{2,10},{3,11},{4,12},{5,13},{6,14},{7,15},{8,0},{9,1},... | collective-permute-start | bytes 393224 | tf_op jit(solution)/shard_map/ppermute | solution.py:13
  32.1 2.5 %collective-permute-start.5 = (f32[256,128]{1,0:T(8,128)S(1)}, f32[256,128]{1,0:T(8,128)S(1)}, u32[]{:S(2)}, u32[]{:S(2)}) collective-permute-start(f32[256,128]{1,0:T(8,128)S(1)} %fusion.14), channel_id=1, source_target_pairs={{0,8},{1,9},{2,10},{3,11},{4,12},{5,13},{6,14},{7,15},{8,0},{9,1},... | collective-permute-start | bytes 393224 | tf_op jit(solution)/shard_map/ppermute | solution.py:13
  34.8 1.8 %collective-permute-done.2 = f32[256,128]{1,0:T(8,128)S(1)} collective-permute-done((f32[256,128]{1,0:T(8,128)S(1)}, f32[256,128]{1,0:T(8,128)S(1)}, u32[]{:S(2)}, u32[]{:S(2)}) %collective-permute-start.2) | collective-permute-done | bytes 131104 | tf_op jit(solution)/shard_map/ppermute | solution.py:13
  36.9 2.5 %collective-permute-start.6 = (f32[256,128]{1,0:T(8,128)S(1)}, f32[256,128]{1,0:T(8,128)S(1)}, u32[]{:S(2)}, u32[]{:S(2)}) collective-permute-start(f32[256,128]{1,0:T(8,128)S(1)} %fusion.13), channel_id=1, source_target_pairs={{0,8},{1,9},{2,10},{3,11},{4,12},{5,13},{6,14},{7,15},{8,0},{9,1},... | collective-permute-start | bytes 393224 | tf_op jit(solution)/shard_map/ppermute | solution.py:13
  39.7 2.5 %collective-permute-done.3 = f32[256,128]{1,0:T(8,128)S(1)} collective-permute-done((f32[256,128]{1,0:T(8,128)S(1)}, f32[256,128]{1,0:T(8,128)S(1)}, u32[]{:S(2)}, u32[]{:S(2)}) %collective-permute-start.3) | collective-permute-done | bytes 131104 | tf_op jit(solution)/shard_map/ppermute | solution.py:13
  42.5 1.9 %collective-permute-start.7 = (f32[256,128]{1,0:T(8,128)S(1)}, f32[256,128]{1,0:T(8,128)S(1)}, u32[]{:S(2)}, u32[]{:S(2)}) collective-permute-start(f32[256,128]{1,0:T(8,128)S(1)} %fusion.12), channel_id=1, source_target_pairs={{0,8},{1,9},{2,10},{3,11},{4,12},{5,13},{6,14},{7,15},{8,0},{9,1},... | collective-permute-start | bytes 393224 | tf_op jit(solution)/shard_map/ppermute | solution.py:13
  44.7 8.2 %collective-permute-done.4 = f32[256,128]{1,0:T(8,128)S(1)} collective-permute-done((f32[256,128]{1,0:T(8,128)S(1)}, f32[256,128]{1,0:T(8,128)S(1)}, u32[]{:S(2)}, u32[]{:S(2)}) %collective-permute-start.4) | collective-permute-done | bytes 131104 | tf_op jit(solution)/shard_map/ppermute | solution.py:13
  53.2 5.9 %collective-permute-start.8 = (f32[256,128]{1,0:T(8,128)S(1)}, f32[256,128]{1,0:T(8,128)S(1)}, u32[]{:S(2)}, u32[]{:S(2)}) collective-permute-start(f32[256,128]{1,0:T(8,128)S(1)} %fusion.11), channel_id=1, source_target_pairs={{0,128},{16,144},{32,160},{48,176},{64,192},{80,208},{96,224},{112... | collective-permute-start | bytes 393224 | tf_op jit(solution)/shard_map/ppermute | solution.py:13
  59.4 0.3 fusion.10
  59.7 3.8 %collective-permute-start.9 = (f32[256,128]{1,0:T(8,128)S(1)}, f32[256,128]{1,0:T(8,128)S(1)}, u32[]{:S(2)}, u32[]{:S(2)}) collective-permute-start(f32[256,128]{1,0:T(8,128)S(1)} %fusion.10), channel_id=1, source_target_pairs={{0,128},{16,144},{32,160},{48,176},{64,192},{80,208},{96,224},{112... | collective-permute-start | bytes 393224 | tf_op jit(solution)/shard_map/ppermute | solution.py:13
  64.1 5.9 %collective-permute-start.10 = (f32[256,128]{1,0:T(8,128)S(1)}, f32[256,128]{1,0:T(8,128)S(1)}, u32[]{:S(2)}, u32[]{:S(2)}) collective-permute-start(f32[256,128]{1,0:T(8,128)S(1)} %fusion.9), channel_id=1, source_target_pairs={{0,128},{16,144},{32,160},{48,176},{64,192},{80,208},{96,224},{112... | collective-permute-start | bytes 393224 | tf_op jit(solution)/shard_map/ppermute | solution.py:13
  70.6 3.8 %collective-permute-start.11 = (f32[256,128]{1,0:T(8,128)S(1)}, f32[256,128]{1,0:T(8,128)S(1)}, u32[]{:S(2)}, u32[]{:S(2)}) collective-permute-start(f32[256,128]{1,0:T(8,128)S(1)} %fusion.8), channel_id=1, source_target_pairs={{0,128},{16,144},{32,160},{48,176},{64,192},{80,208},{96,224},{112... | collective-permute-start | bytes 393224 | tf_op jit(solution)/shard_map/ppermute | solution.py:13
  75.0 1.9 %collective-permute-start.12 = (f32[256,128]{1,0:T(8,128)S(1)}, f32[256,128]{1,0:T(8,128)S(1)}, u32[]{:S(2)}, u32[]{:S(2)}) collective-permute-start(f32[256,128]{1,0:T(8,128)S(1)} %fusion.7), channel_id=1, source_target_pairs={{0,4},{1,5},{2,6},{3,7},{4,0},{5,1},{6,2},{7,3},{8,12},{9,13},{10,... | collective-permute-start | bytes 393224 | tf_op jit(solution)/shard_map/ppermute | solution.py:13
  77.3 0.3 fusion.6
  77.6 3.9 %collective-permute-start.13 = (f32[256,128]{1,0:T(8,128)S(1)}, f32[256,128]{1,0:T(8,128)S(1)}, u32[]{:S(2)}, u32[]{:S(2)}) collective-permute-start(f32[256,128]{1,0:T(8,128)S(1)} %fusion.6), channel_id=1, source_target_pairs={{0,4},{1,5},{2,6},{3,7},{4,0},{5,1},{6,2},{7,3},{8,12},{9,13},{10,... | collective-permute-start | bytes 393224 | tf_op jit(solution)/shard_map/ppermute | solution.py:13
  82.1 1.9 %collective-permute-start.14 = (f32[256,128]{1,0:T(8,128)S(1)}, f32[256,128]{1,0:T(8,128)S(1)}, u32[]{:S(2)}, u32[]{:S(2)}) collective-permute-start(f32[256,128]{1,0:T(8,128)S(1)} %fusion.5), channel_id=1, source_target_pairs={{0,4},{1,5},{2,6},{3,7},{4,0},{5,1},{6,2},{7,3},{8,12},{9,13},{10,... | collective-permute-start | bytes 393224 | tf_op jit(solution)/shard_map/ppermute | solution.py:13
  84.3 1.5 %collective-permute-done.11 = f32[256,128]{1,0:T(8,128)S(1)} collective-permute-done((f32[256,128]{1,0:T(8,128)S(1)}, f32[256,128]{1,0:T(8,128)S(1)}, u32[]{:S(2)}, u32[]{:S(2)}) %collective-permute-start.11) | collective-permute-done | bytes 131104 | tf_op jit(solution)/shard_map/ppermute | solution.py:13
  86.1 2.4 %collective-permute-start.15 = (f32[256,128]{1,0:T(8,128)S(1)}, f32[256,128]{1,0:T(8,128)S(1)}, u32[]{:S(2)}, u32[]{:S(2)}) collective-permute-start(f32[256,128]{1,0:T(8,128)S(1)} %fusion.4), channel_id=1, source_target_pairs={{0,4},{1,5},{2,6},{3,7},{4,0},{5,1},{6,2},{7,3},{8,12},{9,13},{10,... | collective-permute-start | bytes 393224 | tf_op jit(solution)/shard_map/ppermute | solution.py:13
  89.1 0.4 convolution_bitcast_fusion.3
  89.5 0.3 fusion.2
  89.8 0.4 convolution_bitcast_fusion.2
  90.2 0.3 fusion.1
  90.5 0.4 convolution_bitcast_fusion.1
  90.9 2.1 %collective-permute-done.15 = f32[256,128]{1,0:T(8,128)S(1)} collective-permute-done((f32[256,128]{1,0:T(8,128)S(1)}, f32[256,128]{1,0:T(8,128)S(1)}, u32[]{:S(2)}, u32[]{:S(2)}) %collective-permute-start.15) | collective-permute-done | bytes 131104 | tf_op jit(solution)/shard_map/ppermute | solution.py:13
  93.2 0.4 convolution_bitcast_fusion
  93.6 1.0 %maximum_bitcast_fusion = f32[1,1,512,512]{3,2,1,0:T(8,128)} fusion(f32[512,128]{1,0:T(8,128)S(1)} %convolution_bitcast_fusion, f32[512,128]{1,0:T(8,128)S(1)} %convolution_bitcast_fusion.1, f32[512,128]{1,0:T(8,128)S(1)} %convolution_bitcast_fusion.2, f32[512,128]{1,0:T(8,128)S(1)} %convolution_bitcast_fusion.3), kind=kLoop, calls=%fused_computation.52 | loop fusion | flops 786432 | bytes 2097152 | tf_op jit(solution)/shard_map/broadcast_in_dim | solution.py:61
  (46 shorter events, 8.0 us)
Async XLA Ops:
  0.0 1.2 %copy-start = (f32[1,1,512,512]{3,2,1,0:T(8,128)S(1)}, f32[1,1,512,512]{3,2,1,0:T(8,128)}, u32[]{:S(2)}) copy-start(f32[1,1,512,512]{3,2,1,0:T(8,128)} %param.4) | copy-start | bytes 3145732
  0.0 13.9 %copy-start.2 = (f32[1,1,4,256,512]{4,3,2,1,0:T(8,128)S(1)}, f32[1,1,4,256,512]{4,3,2,1,0:T(8,128)}, u32[]{:S(2)}) copy-start(f32[1,1,4,256,512]{4,3,2,1,0:T(8,128)} %param.6) | copy-start | bytes 6291460
  2.9 24.0 %collective-permute-start = (f32[256,128]{1,0:T(8,128)S(1)}, f32[256,128]{1,0:T(8,128)S(1)}, u32[]{:S(2)}, u32[]{:S(2)}) collective-permute-start(f32[256,128]{1,0:T(8,128)S(1)} %get-tuple-element.47), channel_id=1, source_target_pairs={{0,256},{16,272},{32,288},{48,304},{64,320},{80,336},{96,352},{112... | collective-permute-start | bytes 393224 | tf_op jit(solution)/shard_map/ppermute | solution.py:13
  14.3 17.4 %collective-permute-start.1 = (f32[256,128]{1,0:T(8,128)S(1)}, f32[256,128]{1,0:T(8,128)S(1)}, u32[]{:S(2)}, u32[]{:S(2)}) collective-permute-start(f32[256,128]{1,0:T(8,128)S(1)} %get-tuple-element.24), channel_id=1, source_target_pairs={{0,256},{16,272},{32,288},{48,304},{64,320},{80,336},{96,352},{112... | collective-permute-start | bytes 393224 | tf_op jit(solution)/shard_map/ppermute | solution.py:13
  16.6 20.1 %collective-permute-start.2 = (f32[256,128]{1,0:T(8,128)S(1)}, f32[256,128]{1,0:T(8,128)S(1)}, u32[]{:S(2)}, u32[]{:S(2)}) collective-permute-start(f32[256,128]{1,0:T(8,128)S(1)} %get-tuple-element.25), channel_id=1, source_target_pairs={{0,256},{16,272},{32,288},{48,304},{64,320},{80,336},{96,352},{112... | collective-permute-start | bytes 393224 | tf_op jit(solution)/shard_map/ppermute | solution.py:13
  24.7 17.5 %collective-permute-start.3 = (f32[256,128]{1,0:T(8,128)S(1)}, f32[256,128]{1,0:T(8,128)S(1)}, u32[]{:S(2)}, u32[]{:S(2)}) collective-permute-start(f32[256,128]{1,0:T(8,128)S(1)} %get-tuple-element.26), channel_id=1, source_target_pairs={{0,256},{16,272},{32,288},{48,304},{64,320},{80,336},{96,352},{112... | collective-permute-start | bytes 393224 | tf_op jit(solution)/shard_map/ppermute | solution.py:13
  27.2 25.7 %collective-permute-start.4 = (f32[256,128]{1,0:T(8,128)S(1)}, f32[256,128]{1,0:T(8,128)S(1)}, u32[]{:S(2)}, u32[]{:S(2)}) collective-permute-start(f32[256,128]{1,0:T(8,128)S(1)} %fusion.15), channel_id=1, source_target_pairs={{0,8},{1,9},{2,10},{3,11},{4,12},{5,13},{6,14},{7,15},{8,0},{9,1},... | collective-permute-start | bytes 393224 | tf_op jit(solution)/shard_map/ppermute | solution.py:13
  32.1 27.3 %collective-permute-start.5 = (f32[256,128]{1,0:T(8,128)S(1)}, f32[256,128]{1,0:T(8,128)S(1)}, u32[]{:S(2)}, u32[]{:S(2)}) collective-permute-start(f32[256,128]{1,0:T(8,128)S(1)} %fusion.14), channel_id=1, source_target_pairs={{0,8},{1,9},{2,10},{3,11},{4,12},{5,13},{6,14},{7,15},{8,0},{9,1},... | collective-permute-start | bytes 393224 | tf_op jit(solution)/shard_map/ppermute | solution.py:13
  36.9 26.9 %collective-permute-start.6 = (f32[256,128]{1,0:T(8,128)S(1)}, f32[256,128]{1,0:T(8,128)S(1)}, u32[]{:S(2)}, u32[]{:S(2)}) collective-permute-start(f32[256,128]{1,0:T(8,128)S(1)} %fusion.13), channel_id=1, source_target_pairs={{0,8},{1,9},{2,10},{3,11},{4,12},{5,13},{6,14},{7,15},{8,0},{9,1},... | collective-permute-start | bytes 393224 | tf_op jit(solution)/shard_map/ppermute | solution.py:13
  42.5 27.9 %collective-permute-start.7 = (f32[256,128]{1,0:T(8,128)S(1)}, f32[256,128]{1,0:T(8,128)S(1)}, u32[]{:S(2)}, u32[]{:S(2)}) collective-permute-start(f32[256,128]{1,0:T(8,128)S(1)} %fusion.12), channel_id=1, source_target_pairs={{0,8},{1,9},{2,10},{3,11},{4,12},{5,13},{6,14},{7,15},{8,0},{9,1},... | collective-permute-start | bytes 393224 | tf_op jit(solution)/shard_map/ppermute | solution.py:13
  53.2 21.6 %collective-permute-start.8 = (f32[256,128]{1,0:T(8,128)S(1)}, f32[256,128]{1,0:T(8,128)S(1)}, u32[]{:S(2)}, u32[]{:S(2)}) collective-permute-start(f32[256,128]{1,0:T(8,128)S(1)} %fusion.11), channel_id=1, source_target_pairs={{0,128},{16,144},{32,160},{48,176},{64,192},{80,208},{96,224},{112... | collective-permute-start | bytes 393224 | tf_op jit(solution)/shard_map/ppermute | solution.py:13
  59.7 17.6 %collective-permute-start.9 = (f32[256,128]{1,0:T(8,128)S(1)}, f32[256,128]{1,0:T(8,128)S(1)}, u32[]{:S(2)}, u32[]{:S(2)}) collective-permute-start(f32[256,128]{1,0:T(8,128)S(1)} %fusion.10), channel_id=1, source_target_pairs={{0,128},{16,144},{32,160},{48,176},{64,192},{80,208},{96,224},{112... | collective-permute-start | bytes 393224 | tf_op jit(solution)/shard_map/ppermute | solution.py:13
  64.1 17.7 %collective-permute-start.10 = (f32[256,128]{1,0:T(8,128)S(1)}, f32[256,128]{1,0:T(8,128)S(1)}, u32[]{:S(2)}, u32[]{:S(2)}) collective-permute-start(f32[256,128]{1,0:T(8,128)S(1)} %fusion.9), channel_id=1, source_target_pairs={{0,128},{16,144},{32,160},{48,176},{64,192},{80,208},{96,224},{112... | collective-permute-start | bytes 393224 | tf_op jit(solution)/shard_map/ppermute | solution.py:13
  70.6 15.2 %collective-permute-start.11 = (f32[256,128]{1,0:T(8,128)S(1)}, f32[256,128]{1,0:T(8,128)S(1)}, u32[]{:S(2)}, u32[]{:S(2)}) collective-permute-start(f32[256,128]{1,0:T(8,128)S(1)} %fusion.8), channel_id=1, source_target_pairs={{0,128},{16,144},{32,160},{48,176},{64,192},{80,208},{96,224},{112... | collective-permute-start | bytes 393224 | tf_op jit(solution)/shard_map/ppermute | solution.py:13
  75.0 13.8 %collective-permute-start.12 = (f32[256,128]{1,0:T(8,128)S(1)}, f32[256,128]{1,0:T(8,128)S(1)}, u32[]{:S(2)}, u32[]{:S(2)}) collective-permute-start(f32[256,128]{1,0:T(8,128)S(1)} %fusion.7), channel_id=1, source_target_pairs={{0,4},{1,5},{2,6},{3,7},{4,0},{5,1},{6,2},{7,3},{8,12},{9,13},{10,... | collective-permute-start | bytes 393224 | tf_op jit(solution)/shard_map/ppermute | solution.py:13
  77.2 11.8 %copy-start.1 = (f32[1,1,512,256]{3,2,1,0:T(8,128)S(1)}, f32[1,1,512,256]{3,2,1,0:T(8,128)}, u32[]{:S(2)}) copy-start(f32[1,1,512,256]{3,2,1,0:T(8,128)} %param.7) | copy-start | bytes 1572868
  77.6 11.9 %collective-permute-start.13 = (f32[256,128]{1,0:T(8,128)S(1)}, f32[256,128]{1,0:T(8,128)S(1)}, u32[]{:S(2)}, u32[]{:S(2)}) collective-permute-start(f32[256,128]{1,0:T(8,128)S(1)} %fusion.6), channel_id=1, source_target_pairs={{0,4},{1,5},{2,6},{3,7},{4,0},{5,1},{6,2},{7,3},{8,12},{9,13},{10,... | collective-permute-start | bytes 393224 | tf_op jit(solution)/shard_map/ppermute | solution.py:13
  82.1 8.1 %collective-permute-start.14 = (f32[256,128]{1,0:T(8,128)S(1)}, f32[256,128]{1,0:T(8,128)S(1)}, u32[]{:S(2)}, u32[]{:S(2)}) collective-permute-start(f32[256,128]{1,0:T(8,128)S(1)} %fusion.5), channel_id=1, source_target_pairs={{0,4},{1,5},{2,6},{3,7},{4,0},{5,1},{6,2},{7,3},{8,12},{9,13},{10,... | collective-permute-start | bytes 393224 | tf_op jit(solution)/shard_map/ppermute | solution.py:13
  86.1 6.9 %collective-permute-start.15 = (f32[256,128]{1,0:T(8,128)S(1)}, f32[256,128]{1,0:T(8,128)S(1)}, u32[]{:S(2)}, u32[]{:S(2)}) collective-permute-start(f32[256,128]{1,0:T(8,128)S(1)} %fusion.4), channel_id=1, source_target_pairs={{0,4},{1,5},{2,6},{3,7},{4,0},{5,1},{6,2},{7,3},{8,12},{9,13},{10,... | collective-permute-start | bytes 393224 | tf_op jit(solution)/shard_map/ppermute | solution.py:13

commit v2 on v1

--- a/solution.py
+++ b/solution.py
@@ -56,8 +56,9 @@
         else:
             token = pinned(dot(out_basis[0, 0], now))
             out.append((lo, token))
-    out = [x for _, x in sorted(out, key=lambda e: e[0])]
-    result = jnp.concatenate(out, axis=1) if len(out) > 1 else out[0]
+    out = sorted(out, key=lambda e: e[0])
+    early = [x for _, x in out[:-1]] + [jnp.zeros_like(out[-1][1])]
+    result = lax.dynamic_update_slice(jnp.concatenate(early, axis=1), out[-1][1], (0, out[-1][0] * width))
     return result[None, None]
 
 

time: 95.2 us -> 94.9 us (level)
  waiting for transfers between devices: 16.1 us -> 15 us
    ppermute x16, waiting for transfers between devices: 16.1 us -> 15 us  [swapped(): lax.ppermute(x, axis, [(i, i ^ 1 << apart) for i in range(lax.axis_size(a...]
  transfers between devices with their start and end apart: 16 -> 16, of which waited for: 5 -> 5; matrix products, arithmetic and copies ran while one was open for 11% -> 12% of each run, Pallas kernels for 0% -> 0%
where the time goes in v2:
time: 94.9 us; the launch traced here: 94.3 us
  starting transfers between devices  63.4 us (67%)
  waiting for transfers between devices  15 us (16%)
  matrix products  12.8 us (13%)
  local copies, waits for them, and re-layouts  1.45 us (2%)
  other arithmetic  1.11 us (1%)
    ppermute x16, starting transfers between devices, swapped(): lax.ppermute(x, axis, [(i, i ^ 1 << apart) for i in range(lax.axis_size(a...  63.4 us
    ppermute x16, waiting for transfers between devices, swapped(): lax.ppermute(x, axis, [(i, i ^ 1 << apart) for i in range(lax.axis_size(a...  15 us
    dot_general x36, matrix products, dot(): return jnp.dot(a, b, precision=HIGH, preferred_element_type=jnp.float32)  11.2 us
  transfers between devices with their start and end apart: 16, of which 5 were waited for; matrix products, arithmetic and copies ran while one was open for 12% of the time, Pallas kernels for 0%

profile of v2, /device:TPU:18, one launch (start us, length us, event | category | flops | bytes accessed | tf_op | source)
XLA Modules:
  0.0 94.3 jit_solution(3913449216070513405)
XLA Ops:
  0.0 1.2 %copy-done = f32[1,1,512,512]{3,2,1,0:T(8,128)S(1)} copy-done((f32[1,1,512,512]{3,2,1,0:T(8,128)S(1)}, f32[1,1,512,512]{3,2,1,0:T(8,128)}, u32[]{:S(2)}) %copy-start) | copy-done | bytes 1048600
  1.2 1.7 %fusion.17 = f32[256,512]{1,0:T(8,128)S(1)} fusion(f32[1,1,512,512]{3,2,1,0:T(8,128)S(1)} %copy-done, f32[1,1,512,256]{3,2,1,0:T(8,128)} %param.5), kind=kOutput, calls=%fused_computation.54 | convolution fusion | flops 402653184 | bytes 2097152 | tf_op jit(solution)/shard_map/mk,mr->kr/dot_general | solution.py:35
  2.9 10.9 %collective-permute-start = (f32[256,128]{1,0:T(8,128)S(1)}, f32[256,128]{1,0:T(8,128)S(1)}, u32[]{:S(2)}, u32[]{:S(2)}) collective-permute-start(f32[256,128]{1,0:T(8,128)S(1)} %get-tuple-element.47), channel_id=1, source_target_pairs={{0,256},{16,272},{32,288},{48,304},{64,320},{80,336},{96,352},{112... | collective-permute-start | bytes 393224 | tf_op jit(solution)/shard_map/ppermute | solution.py:13
  14.3 1.9 %collective-permute-start.1 = (f32[256,128]{1,0:T(8,128)S(1)}, f32[256,128]{1,0:T(8,128)S(1)}, u32[]{:S(2)}, u32[]{:S(2)}) collective-permute-start(f32[256,128]{1,0:T(8,128)S(1)} %get-tuple-element.24), channel_id=1, source_target_pairs={{0,256},{16,272},{32,288},{48,304},{64,320},{80,336},{96,352},{112... | collective-permute-start | bytes 393224 | tf_op jit(solution)/shard_map/ppermute | solution.py:13
  16.6 7.8 %collective-permute-start.2 = (f32[256,128]{1,0:T(8,128)S(1)}, f32[256,128]{1,0:T(8,128)S(1)}, u32[]{:S(2)}, u32[]{:S(2)}) collective-permute-start(f32[256,128]{1,0:T(8,128)S(1)} %get-tuple-element.25), channel_id=1, source_target_pairs={{0,256},{16,272},{32,288},{48,304},{64,320},{80,336},{96,352},{112... | collective-permute-start | bytes 393224 | tf_op jit(solution)/shard_map/ppermute | solution.py:13
  24.7 1.9 %collective-permute-start.3 = (f32[256,128]{1,0:T(8,128)S(1)}, f32[256,128]{1,0:T(8,128)S(1)}, u32[]{:S(2)}, u32[]{:S(2)}) collective-permute-start(f32[256,128]{1,0:T(8,128)S(1)} %get-tuple-element.26), channel_id=1, source_target_pairs={{0,256},{16,272},{32,288},{48,304},{64,320},{80,336},{96,352},{112... | collective-permute-start | bytes 393224 | tf_op jit(solution)/shard_map/ppermute | solution.py:13
  27.2 4.3 %collective-permute-start.4 = (f32[256,128]{1,0:T(8,128)S(1)}, f32[256,128]{1,0:T(8,128)S(1)}, u32[]{:S(2)}, u32[]{:S(2)}) collective-permute-start(f32[256,128]{1,0:T(8,128)S(1)} %fusion.16), channel_id=1, source_target_pairs={{0,8},{1,9},{2,10},{3,11},{4,12},{5,13},{6,14},{7,15},{8,0},{9,1},... | collective-permute-start | bytes 393224 | tf_op jit(solution)/shard_map/ppermute | solution.py:13
  32.1 2.5 %collective-permute-start.5 = (f32[256,128]{1,0:T(8,128)S(1)}, f32[256,128]{1,0:T(8,128)S(1)}, u32[]{:S(2)}, u32[]{:S(2)}) collective-permute-start(f32[256,128]{1,0:T(8,128)S(1)} %fusion.15), channel_id=1, source_target_pairs={{0,8},{1,9},{2,10},{3,11},{4,12},{5,13},{6,14},{7,15},{8,0},{9,1},... | collective-permute-start | bytes 393224 | tf_op jit(solution)/shard_map/ppermute | solution.py:13
  34.8 1.8 %collective-permute-done.2 = f32[256,128]{1,0:T(8,128)S(1)} collective-permute-done((f32[256,128]{1,0:T(8,128)S(1)}, f32[256,128]{1,0:T(8,128)S(1)}, u32[]{:S(2)}, u32[]{:S(2)}) %collective-permute-start.2) | collective-permute-done | bytes 131104 | tf_op jit(solution)/shard_map/ppermute | solution.py:13
  36.9 2.5 %collective-permute-start.6 = (f32[256,128]{1,0:T(8,128)S(1)}, f32[256,128]{1,0:T(8,128)S(1)}, u32[]{:S(2)}, u32[]{:S(2)}) collective-permute-start(f32[256,128]{1,0:T(8,128)S(1)} %fusion.14), channel_id=1, source_target_pairs={{0,8},{1,9},{2,10},{3,11},{4,12},{5,13},{6,14},{7,15},{8,0},{9,1},... | collective-permute-start | bytes 393224 | tf_op jit(solution)/shard_map/ppermute | solution.py:13
  39.7 2.5 %collective-permute-done.3 = f32[256,128]{1,0:T(8,128)S(1)} collective-permute-done((f32[256,128]{1,0:T(8,128)S(1)}, f32[256,128]{1,0:T(8,128)S(1)}, u32[]{:S(2)}, u32[]{:S(2)}) %collective-permute-start.3) | collective-permute-done | bytes 131104 | tf_op jit(solution)/shard_map/ppermute | solution.py:13
  42.5 1.9 %collective-permute-start.7 = (f32[256,128]{1,0:T(8,128)S(1)}, f32[256,128]{1,0:T(8,128)S(1)}, u32[]{:S(2)}, u32[]{:S(2)}) collective-permute-start(f32[256,128]{1,0:T(8,128)S(1)} %fusion.13), channel_id=1, source_target_pairs={{0,8},{1,9},{2,10},{3,11},{4,12},{5,13},{6,14},{7,15},{8,0},{9,1},... | collective-permute-start | bytes 393224 | tf_op jit(solution)/shard_map/ppermute | solution.py:13
  44.7 8.2 %collective-permute-done.4 = f32[256,128]{1,0:T(8,128)S(1)} collective-permute-done((f32[256,128]{1,0:T(8,128)S(1)}, f32[256,128]{1,0:T(8,128)S(1)}, u32[]{:S(2)}, u32[]{:S(2)}) %collective-permute-start.4) | collective-permute-done | bytes 131104 | tf_op jit(solution)/shard_map/ppermute | solution.py:13
  53.2 5.9 %collective-permute-start.8 = (f32[256,128]{1,0:T(8,128)S(1)}, f32[256,128]{1,0:T(8,128)S(1)}, u32[]{:S(2)}, u32[]{:S(2)}) collective-permute-start(f32[256,128]{1,0:T(8,128)S(1)} %fusion.12), channel_id=1, source_target_pairs={{0,128},{16,144},{32,160},{48,176},{64,192},{80,208},{96,224},{112... | collective-permute-start | bytes 393224 | tf_op jit(solution)/shard_map/ppermute | solution.py:13
  59.7 3.8 %collective-permute-start.9 = (f32[256,128]{1,0:T(8,128)S(1)}, f32[256,128]{1,0:T(8,128)S(1)}, u32[]{:S(2)}, u32[]{:S(2)}) collective-permute-start(f32[256,128]{1,0:T(8,128)S(1)} %fusion.11), channel_id=1, source_target_pairs={{0,128},{16,144},{32,160},{48,176},{64,192},{80,208},{96,224},{112... | collective-permute-start | bytes 393224 | tf_op jit(solution)/shard_map/ppermute | solution.py:13
  63.5 0.3 convolution_bitcast_fusion.20
  64.1 5.9 %collective-permute-start.10 = (f32[256,128]{1,0:T(8,128)S(1)}, f32[256,128]{1,0:T(8,128)S(1)}, u32[]{:S(2)}, u32[]{:S(2)}) collective-permute-start(f32[256,128]{1,0:T(8,128)S(1)} %fusion.10), channel_id=1, source_target_pairs={{0,128},{16,144},{32,160},{48,176},{64,192},{80,208},{96,224},{112... | collective-permute-start | bytes 393224 | tf_op jit(solution)/shard_map/ppermute | solution.py:13
  70.0 0.3 convolution_bitcast_fusion.18
  70.6 3.8 %collective-permute-start.11 = (f32[256,128]{1,0:T(8,128)S(1)}, f32[256,128]{1,0:T(8,128)S(1)}, u32[]{:S(2)}, u32[]{:S(2)}) collective-permute-start(f32[256,128]{1,0:T(8,128)S(1)} %fusion.9), channel_id=1, source_target_pairs={{0,128},{16,144},{32,160},{48,176},{64,192},{80,208},{96,224},{112... | collective-permute-start | bytes 393224 | tf_op jit(solution)/shard_map/ppermute | solution.py:13
  75.0 1.9 %collective-permute-start.12 = (f32[256,128]{1,0:T(8,128)S(1)}, f32[256,128]{1,0:T(8,128)S(1)}, u32[]{:S(2)}, u32[]{:S(2)}) collective-permute-start(f32[256,128]{1,0:T(8,128)S(1)} %fusion.8), channel_id=1, source_target_pairs={{0,4},{1,5},{2,6},{3,7},{4,0},{5,1},{6,2},{7,3},{8,12},{9,13},{10,... | collective-permute-start | bytes 393224 | tf_op jit(solution)/shard_map/ppermute | solution.py:13
  77.0 0.3 convolution_bitcast_fusion.14
  77.5 3.9 %collective-permute-start.13 = (f32[256,128]{1,0:T(8,128)S(1)}, f32[256,128]{1,0:T(8,128)S(1)}, u32[]{:S(2)}, u32[]{:S(2)}) collective-permute-start(f32[256,128]{1,0:T(8,128)S(1)} %fusion.7), channel_id=1, source_target_pairs={{0,4},{1,5},{2,6},{3,7},{4,0},{5,1},{6,2},{7,3},{8,12},{9,13},{10,... | collective-permute-start | bytes 393224 | tf_op jit(solution)/shard_map/ppermute | solution.py:13
  82.1 1.9 %collective-permute-start.14 = (f32[256,128]{1,0:T(8,128)S(1)}, f32[256,128]{1,0:T(8,128)S(1)}, u32[]{:S(2)}, u32[]{:S(2)}) collective-permute-start(f32[256,128]{1,0:T(8,128)S(1)} %fusion.6), channel_id=1, source_target_pairs={{0,4},{1,5},{2,6},{3,7},{4,0},{5,1},{6,2},{7,3},{8,12},{9,13},{10,... | collective-permute-start | bytes 393224 | tf_op jit(solution)/shard_map/ppermute | solution.py:13
  84.0 0.3 convolution_bitcast_fusion.10
  84.3 1.5 %collective-permute-done.11 = f32[256,128]{1,0:T(8,128)S(1)} collective-permute-done((f32[256,128]{1,0:T(8,128)S(1)}, f32[256,128]{1,0:T(8,128)S(1)}, u32[]{:S(2)}, u32[]{:S(2)}) %collective-permute-start.11) | collective-permute-done | bytes 131104 | tf_op jit(solution)/shard_map/ppermute | solution.py:13
  86.1 2.4 %collective-permute-start.15 = (f32[256,128]{1,0:T(8,128)S(1)}, f32[256,128]{1,0:T(8,128)S(1)}, u32[]{:S(2)}, u32[]{:S(2)}) collective-permute-start(f32[256,128]{1,0:T(8,128)S(1)} %fusion.5), channel_id=1, source_target_pairs={{0,4},{1,5},{2,6},{3,7},{4,0},{5,1},{6,2},{7,3},{8,12},{9,13},{10,... | collective-permute-start | bytes 393224 | tf_op jit(solution)/shard_map/ppermute | solution.py:13
  89.1 0.4 convolution_bitcast_fusion.3
  89.8 0.4 convolution_bitcast_fusion.2
  90.5 0.4 convolution_bitcast_fusion.1
  90.9 1.1 %maximum_bitcast_fusion = f32[1,1,512,512]{3,2,1,0:T(8,128)} fusion(f32[512,128]{1,0:T(8,128)S(1)} %convolution_bitcast_fusion.1, f32[512,128]{1,0:T(8,128)S(1)} %convolution_bitcast_fusion.2, f32[512,128]{1,0:T(8,128)S(1)} %convolution_bitcast_fusion.3, f32[512]{0:T(512)S(1)} %pad.3.clone), kind=kLoop, calls=%fused_computation.53 | loop fusion | flops 786432 | bytes 1837056 | tf_op jit(solution)/shard_map/broadcast_in_dim | solution.py:62
  92.0 1.0 %collective-permute-done.15 = f32[256,128]{1,0:T(8,128)S(1)} collective-permute-done((f32[256,128]{1,0:T(8,128)S(1)}, f32[256,128]{1,0:T(8,128)S(1)}, u32[]{:S(2)}, u32[]{:S(2)}) %collective-permute-start.15) | collective-permute-done | bytes 131104 | tf_op jit(solution)/shard_map/ppermute | solution.py:13
  93.2 1.1 %fusion = f32[1,1,512,512]{3,2,1,0:T(8,128)} fusion(f32[1,1,512,512]{3,2,1,0:T(8,128)} %maximum_bitcast_fusion, f32[256,128]{1,0:T(8,128)S(1)} %fusion.1, f32[1,1,512,256]{3,2,1,0:T(8,128)S(1)} %copy-done.1), kind=kOutput, calls=%fused_computation.1 | convolution fusion | flops 100663296 | bytes 917504 | tf_op jit(solution)/shard_map/dot_general | solution.py:17
  (48 shorter events, 8.0 us)
Async XLA Ops:
  0.0 1.2 %copy-start = (f32[1,1,512,512]{3,2,1,0:T(8,128)S(1)}, f32[1,1,512,512]{3,2,1,0:T(8,128)}, u32[]{:S(2)}) copy-start(f32[1,1,512,512]{3,2,1,0:T(8,128)} %param.4) | copy-start | bytes 3145732
  0.0 13.9 %copy-start.2 = (f32[1,1,4,256,512]{4,3,2,1,0:T(8,128)S(1)}, f32[1,1,4,256,512]{4,3,2,1,0:T(8,128)}, u32[]{:S(2)}) copy-start(f32[1,1,4,256,512]{4,3,2,1,0:T(8,128)} %param.6) | copy-start | bytes 6291460
  2.9 24.0 %collective-permute-start = (f32[256,128]{1,0:T(8,128)S(1)}, f32[256,128]{1,0:T(8,128)S(1)}, u32[]{:S(2)}, u32[]{:S(2)}) collective-permute-start(f32[256,128]{1,0:T(8,128)S(1)} %get-tuple-element.47), channel_id=1, source_target_pairs={{0,256},{16,272},{32,288},{48,304},{64,320},{80,336},{96,352},{112... | collective-permute-start | bytes 393224 | tf_op jit(solution)/shard_map/ppermute | solution.py:13
  14.3 17.5 %collective-permute-start.1 = (f32[256,128]{1,0:T(8,128)S(1)}, f32[256,128]{1,0:T(8,128)S(1)}, u32[]{:S(2)}, u32[]{:S(2)}) collective-permute-start(f32[256,128]{1,0:T(8,128)S(1)} %get-tuple-element.24), channel_id=1, source_target_pairs={{0,256},{16,272},{32,288},{48,304},{64,320},{80,336},{96,352},{112... | collective-permute-start | bytes 393224 | tf_op jit(solution)/shard_map/ppermute | solution.py:13
  16.6 20.1 %collective-permute-start.2 = (f32[256,128]{1,0:T(8,128)S(1)}, f32[256,128]{1,0:T(8,128)S(1)}, u32[]{:S(2)}, u32[]{:S(2)}) collective-permute-start(f32[256,128]{1,0:T(8,128)S(1)} %get-tuple-element.25), channel_id=1, source_target_pairs={{0,256},{16,272},{32,288},{48,304},{64,320},{80,336},{96,352},{112... | collective-permute-start | bytes 393224 | tf_op jit(solution)/shard_map/ppermute | solution.py:13
  24.7 17.5 %collective-permute-start.3 = (f32[256,128]{1,0:T(8,128)S(1)}, f32[256,128]{1,0:T(8,128)S(1)}, u32[]{:S(2)}, u32[]{:S(2)}) collective-permute-start(f32[256,128]{1,0:T(8,128)S(1)} %get-tuple-element.26), channel_id=1, source_target_pairs={{0,256},{16,272},{32,288},{48,304},{64,320},{80,336},{96,352},{112... | collective-permute-start | bytes 393224 | tf_op jit(solution)/shard_map/ppermute | solution.py:13
  27.2 25.7 %collective-permute-start.4 = (f32[256,128]{1,0:T(8,128)S(1)}, f32[256,128]{1,0:T(8,128)S(1)}, u32[]{:S(2)}, u32[]{:S(2)}) collective-permute-start(f32[256,128]{1,0:T(8,128)S(1)} %fusion.16), channel_id=1, source_target_pairs={{0,8},{1,9},{2,10},{3,11},{4,12},{5,13},{6,14},{7,15},{8,0},{9,1},... | collective-permute-start | bytes 393224 | tf_op jit(solution)/shard_map/ppermute | solution.py:13
  32.1 27.3 %collective-permute-start.5 = (f32[256,128]{1,0:T(8,128)S(1)}, f32[256,128]{1,0:T(8,128)S(1)}, u32[]{:S(2)}, u32[]{:S(2)}) collective-permute-start(f32[256,128]{1,0:T(8,128)S(1)} %fusion.15), channel_id=1, source_target_pairs={{0,8},{1,9},{2,10},{3,11},{4,12},{5,13},{6,14},{7,15},{8,0},{9,1},... | collective-permute-start | bytes 393224 | tf_op jit(solution)/shard_map/ppermute | solution.py:13
  36.9 26.9 %collective-permute-start.6 = (f32[256,128]{1,0:T(8,128)S(1)}, f32[256,128]{1,0:T(8,128)S(1)}, u32[]{:S(2)}, u32[]{:S(2)}) collective-permute-start(f32[256,128]{1,0:T(8,128)S(1)} %fusion.14), channel_id=1, source_target_pairs={{0,8},{1,9},{2,10},{3,11},{4,12},{5,13},{6,14},{7,15},{8,0},{9,1},... | collective-permute-start | bytes 393224 | tf_op jit(solution)/shard_map/ppermute | solution.py:13
  42.5 27.9 %collective-permute-start.7 = (f32[256,128]{1,0:T(8,128)S(1)}, f32[256,128]{1,0:T(8,128)S(1)}, u32[]{:S(2)}, u32[]{:S(2)}) collective-permute-start(f32[256,128]{1,0:T(8,128)S(1)} %fusion.13), channel_id=1, source_target_pairs={{0,8},{1,9},{2,10},{3,11},{4,12},{5,13},{6,14},{7,15},{8,0},{9,1},... | collective-permute-start | bytes 393224 | tf_op jit(solution)/shard_map/ppermute | solution.py:13
  53.2 21.6 %collective-permute-start.8 = (f32[256,128]{1,0:T(8,128)S(1)}, f32[256,128]{1,0:T(8,128)S(1)}, u32[]{:S(2)}, u32[]{:S(2)}) collective-permute-start(f32[256,128]{1,0:T(8,128)S(1)} %fusion.12), channel_id=1, source_target_pairs={{0,128},{16,144},{32,160},{48,176},{64,192},{80,208},{96,224},{112... | collective-permute-start | bytes 393224 | tf_op jit(solution)/shard_map/ppermute | solution.py:13
  59.7 17.6 %collective-permute-start.9 = (f32[256,128]{1,0:T(8,128)S(1)}, f32[256,128]{1,0:T(8,128)S(1)}, u32[]{:S(2)}, u32[]{:S(2)}) collective-permute-start(f32[256,128]{1,0:T(8,128)S(1)} %fusion.11), channel_id=1, source_target_pairs={{0,128},{16,144},{32,160},{48,176},{64,192},{80,208},{96,224},{112... | collective-permute-start | bytes 393224 | tf_op jit(solution)/shard_map/ppermute | solution.py:13
  64.1 17.7 %collective-permute-start.10 = (f32[256,128]{1,0:T(8,128)S(1)}, f32[256,128]{1,0:T(8,128)S(1)}, u32[]{:S(2)}, u32[]{:S(2)}) collective-permute-start(f32[256,128]{1,0:T(8,128)S(1)} %fusion.10), channel_id=1, source_target_pairs={{0,128},{16,144},{32,160},{48,176},{64,192},{80,208},{96,224},{112... | collective-permute-start | bytes 393224 | tf_op jit(solution)/shard_map/ppermute | solution.py:13
  70.6 15.2 %collective-permute-start.11 = (f32[256,128]{1,0:T(8,128)S(1)}, f32[256,128]{1,0:T(8,128)S(1)}, u32[]{:S(2)}, u32[]{:S(2)}) collective-permute-start(f32[256,128]{1,0:T(8,128)S(1)} %fusion.9), channel_id=1, source_target_pairs={{0,128},{16,144},{32,160},{48,176},{64,192},{80,208},{96,224},{112... | collective-permute-start | bytes 393224 | tf_op jit(solution)/shard_map/ppermute | solution.py:13
  75.0 13.8 %collective-permute-start.12 = (f32[256,128]{1,0:T(8,128)S(1)}, f32[256,128]{1,0:T(8,128)S(1)}, u32[]{:S(2)}, u32[]{:S(2)}) collective-permute-start(f32[256,128]{1,0:T(8,128)S(1)} %fusion.8), channel_id=1, source_target_pairs={{0,4},{1,5},{2,6},{3,7},{4,0},{5,1},{6,2},{7,3},{8,12},{9,13},{10,... | collective-permute-start | bytes 393224 | tf_op jit(solution)/shard_map/ppermute | solution.py:13
  77.2 11.8 %copy-start.1 = (f32[1,1,512,256]{3,2,1,0:T(8,128)S(1)}, f32[1,1,512,256]{3,2,1,0:T(8,128)}, u32[]{:S(2)}) copy-start(f32[1,1,512,256]{3,2,1,0:T(8,128)} %param.7) | copy-start | bytes 1572868
  77.5 11.9 %collective-permute-start.13 = (f32[256,128]{1,0:T(8,128)S(1)}, f32[256,128]{1,0:T(8,128)S(1)}, u32[]{:S(2)}, u32[]{:S(2)}) collective-permute-start(f32[256,128]{1,0:T(8,128)S(1)} %fusion.7), channel_id=1, source_target_pairs={{0,4},{1,5},{2,6},{3,7},{4,0},{5,1},{6,2},{7,3},{8,12},{9,13},{10,... | collective-permute-start | bytes 393224 | tf_op jit(solution)/shard_map/ppermute | solution.py:13
  82.1 8.1 %collective-permute-start.14 = (f32[256,128]{1,0:T(8,128)S(1)}, f32[256,128]{1,0:T(8,128)S(1)}, u32[]{:S(2)}, u32[]{:S(2)}) collective-permute-start(f32[256,128]{1,0:T(8,128)S(1)} %fusion.6), channel_id=1, source_target_pairs={{0,4},{1,5},{2,6},{3,7},{4,0},{5,1},{6,2},{7,3},{8,12},{9,13},{10,... | collective-permute-start | bytes 393224 | tf_op jit(solution)/shard_map/ppermute | solution.py:13
  86.1 6.9 %collective-permute-start.15 = (f32[256,128]{1,0:T(8,128)S(1)}, f32[256,128]{1,0:T(8,128)S(1)}, u32[]{:S(2)}, u32[]{:S(2)}) collective-permute-start(f32[256,128]{1,0:T(8,128)S(1)} %fusion.5), channel_id=1, source_target_pairs={{0,4},{1,5},{2,6},{3,7},{4,0},{5,1},{6,2},{7,3},{8,12},{9,13},{10,... | collective-permute-start | bytes 393224 | tf_op jit(solution)/shard_map/ppermute | solution.py:13

commit v3 on v2

--- a/solution.py
+++ b/solution.py
@@ -33,13 +33,12 @@
         return swapped(x, "col", col_bits - 1 - level // 2)
 
     coeff = jnp.einsum("mk,mr->kr", leaf_basis[0, 0], sources[0, 0], precision=HIGH, preferred_element_type=jnp.float32)
+    every = dot(transfers[0, 0, 0][:, :rank], coeff)
     sent = [[] for _ in range(levels)]
     out, token = [], None
     for level, lo, hi in STEPS:
         if level == 0:
             now = coeff[:, lo * width:hi * width]
-            if token is not None:
-                now, token = lax.optimization_barrier((now, token))
         else:
             pieces = []
             for a, b, own, other in sent[level - 1]:
@@ -50,9 +49,9 @@
                     pieces.append(kept + dot(transfers[0, 0, level - 1][:, rank:], other[:, cut]))
             now = pinned(jnp.concatenate(pieces, axis=1) if len(pieces) > 1 else pieces[0])
         if level < levels:
-            own = dot(transfers[0, 0, level][:, :rank], now)
+            own = every[:, lo * width:hi * width] if level == 0 else dot(transfers[0, 0, level][:, :rank], now)
             sent[level].append((lo, hi, own, partner(now, level)))
-            token = own
+            token = every if level == 0 else own
         else:
             token = pinned(dot(out_basis[0, 0], now))
             out.append((lo, token))

time: 94.9 us -> 94.4 us (level)
    dot_general x36 -> x33, matrix products: 11.2 us -> 10.5 us  [dot(): return jnp.dot(a, b, precision=HIGH, preferred_element_type=jnp.float32)]
  transfers between devices with their start and end apart: 16 -> 16, of which waited for: 5 -> 5; matrix products, arithmetic and copies ran while one was open for 12% -> 11% of each run, Pallas kernels for 0% -> 0%
where the time goes in v3:
time: 94.4 us; the launch traced here: 93.8 us
  starting transfers between devices  62.8 us (67%)
  waiting for transfers between devices  15.7 us (17%)
  matrix products  12.2 us (13%)
  local copies, waits for them, and re-layouts  1.49 us (2%)
  other arithmetic  1.11 us (1%)
    ppermute x16, starting transfers between devices, swapped(): lax.ppermute(x, axis, [(i, i ^ 1 << apart) for i in range(lax.axis_size(a...  62.8 us
    ppermute x16, waiting for transfers between devices, swapped(): lax.ppermute(x, axis, [(i, i ^ 1 << apart) for i in range(lax.axis_size(a...  15.7 us
    dot_general x33, matrix products, dot(): return jnp.dot(a, b, precision=HIGH, preferred_element_type=jnp.float32)  10.5 us
  transfers between devices with their start and end apart: 16, of which 5 were waited for; matrix products, arithmetic and copies ran while one was open for 11% of the time, Pallas kernels for 0%

profile of v3, /device:TPU:18, one launch (start us, length us, event | category | flops | bytes accessed | tf_op | source)
XLA Modules:
  0.0 93.8 jit_solution(6684360460443777558)
XLA Ops:
  0.0 1.2 %copy-done = f32[1,1,512,512]{3,2,1,0:T(8,128)S(1)} copy-done((f32[1,1,512,512]{3,2,1,0:T(8,128)S(1)}, f32[1,1,512,512]{3,2,1,0:T(8,128)}, u32[]{:S(2)}) %copy-start) | copy-done | bytes 1048600
  1.2 1.7 %fusion.17 = f32[256,512]{1,0:T(8,128)S(1)} fusion(f32[1,1,512,512]{3,2,1,0:T(8,128)S(1)} %copy-done, f32[1,1,512,256]{3,2,1,0:T(8,128)} %param.5), kind=kOutput, calls=%fused_computation.51 | convolution fusion | flops 402653184 | bytes 2097152 | tf_op jit(solution)/shard_map/mk,mr->kr/dot_general | solution.py:35
  2.9 10.9 %collective-permute-start = (f32[256,128]{1,0:T(8,128)S(1)}, f32[256,128]{1,0:T(8,128)S(1)}, u32[]{:S(2)}, u32[]{:S(2)}) collective-permute-start(f32[256,128]{1,0:T(8,128)S(1)} %get-tuple-element.44), channel_id=1, source_target_pairs={{0,256},{16,272},{32,288},{48,304},{64,320},{80,336},{96,352},{112... | collective-permute-start | bytes 393224 | tf_op jit(solution)/shard_map/ppermute | solution.py:13
  13.9 1.9 %collective-permute-start.1 = (f32[256,128]{1,0:T(8,128)S(1)}, f32[256,128]{1,0:T(8,128)S(1)}, u32[]{:S(2)}, u32[]{:S(2)}) collective-permute-start(f32[256,128]{1,0:T(8,128)S(1)} %get-tuple-element.43), channel_id=1, source_target_pairs={{0,256},{16,272},{32,288},{48,304},{64,320},{80,336},{96,352},{112... | collective-permute-start | bytes 393224 | tf_op jit(solution)/shard_map/ppermute | solution.py:13
  15.8 7.8 %collective-permute-start.2 = (f32[256,128]{1,0:T(8,128)S(1)}, f32[256,128]{1,0:T(8,128)S(1)}, u32[]{:S(2)}, u32[]{:S(2)}) collective-permute-start(f32[256,128]{1,0:T(8,128)S(1)} %get-tuple-element.42), channel_id=1, source_target_pairs={{0,256},{16,272},{32,288},{48,304},{64,320},{80,336},{96,352},{112... | collective-permute-start | bytes 393224 | tf_op jit(solution)/shard_map/ppermute | solution.py:13
  23.6 1.9 %collective-permute-start.3 = (f32[256,128]{1,0:T(8,128)S(1)}, f32[256,128]{1,0:T(8,128)S(1)}, u32[]{:S(2)}, u32[]{:S(2)}) collective-permute-start(f32[256,128]{1,0:T(8,128)S(1)} %get-tuple-element.41), channel_id=1, source_target_pairs={{0,256},{16,272},{32,288},{48,304},{64,320},{80,336},{96,352},{112... | collective-permute-start | bytes 393224 | tf_op jit(solution)/shard_map/ppermute | solution.py:13
  25.7 0.4 convolution_bitcast_fusion
  26.5 4.3 %collective-permute-start.4 = (f32[256,128]{1,0:T(8,128)S(1)}, f32[256,128]{1,0:T(8,128)S(1)}, u32[]{:S(2)}, u32[]{:S(2)}) collective-permute-start(f32[256,128]{1,0:T(8,128)S(1)} %fusion.16), channel_id=1, source_target_pairs={{0,8},{1,9},{2,10},{3,11},{4,12},{5,13},{6,14},{7,15},{8,0},{9,1},... | collective-permute-start | bytes 393224 | tf_op jit(solution)/shard_map/ppermute | solution.py:13
  31.4 2.5 %collective-permute-start.5 = (f32[256,128]{1,0:T(8,128)S(1)}, f32[256,128]{1,0:T(8,128)S(1)}, u32[]{:S(2)}, u32[]{:S(2)}) collective-permute-start(f32[256,128]{1,0:T(8,128)S(1)} %fusion.15), channel_id=1, source_target_pairs={{0,8},{1,9},{2,10},{3,11},{4,12},{5,13},{6,14},{7,15},{8,0},{9,1},... | collective-permute-start | bytes 393224 | tf_op jit(solution)/shard_map/ppermute | solution.py:13
  34.2 2.6 %collective-permute-done.2 = f32[256,128]{1,0:T(8,128)S(1)} collective-permute-done((f32[256,128]{1,0:T(8,128)S(1)}, f32[256,128]{1,0:T(8,128)S(1)}, u32[]{:S(2)}, u32[]{:S(2)}) %collective-permute-start.2) | collective-permute-done | bytes 131104 | tf_op jit(solution)/shard_map/ppermute | solution.py:13
  37.1 1.9 %collective-permute-start.6 = (f32[256,128]{1,0:T(8,128)S(1)}, f32[256,128]{1,0:T(8,128)S(1)}, u32[]{:S(2)}, u32[]{:S(2)}) collective-permute-start(f32[256,128]{1,0:T(8,128)S(1)} %fusion.14), channel_id=1, source_target_pairs={{0,8},{1,9},{2,10},{3,11},{4,12},{5,13},{6,14},{7,15},{8,0},{9,1},... | collective-permute-start | bytes 393224 | tf_op jit(solution)/shard_map/ppermute | solution.py:13
  39.3 3.0 %collective-permute-done.3 = f32[256,128]{1,0:T(8,128)S(1)} collective-permute-done((f32[256,128]{1,0:T(8,128)S(1)}, f32[256,128]{1,0:T(8,128)S(1)}, u32[]{:S(2)}, u32[]{:S(2)}) %collective-permute-start.3) | collective-permute-done | bytes 131104 | tf_op jit(solution)/shard_map/ppermute | solution.py:13
  42.5 1.9 %collective-permute-start.7 = (f32[256,128]{1,0:T(8,128)S(1)}, f32[256,128]{1,0:T(8,128)S(1)}, u32[]{:S(2)}, u32[]{:S(2)}) collective-permute-start(f32[256,128]{1,0:T(8,128)S(1)} %fusion.13), channel_id=1, source_target_pairs={{0,8},{1,9},{2,10},{3,11},{4,12},{5,13},{6,14},{7,15},{8,0},{9,1},... | collective-permute-start | bytes 393224 | tf_op jit(solution)/shard_map/ppermute | solution.py:13
  44.7 7.6 %collective-permute-done.4 = f32[256,128]{1,0:T(8,128)S(1)} collective-permute-done((f32[256,128]{1,0:T(8,128)S(1)}, f32[256,128]{1,0:T(8,128)S(1)}, u32[]{:S(2)}, u32[]{:S(2)}) %collective-permute-start.4) | collective-permute-done | bytes 131104 | tf_op jit(solution)/shard_map/ppermute | solution.py:13
  52.6 5.9 %collective-permute-start.8 = (f32[256,128]{1,0:T(8,128)S(1)}, f32[256,128]{1,0:T(8,128)S(1)}, u32[]{:S(2)}, u32[]{:S(2)}) collective-permute-start(f32[256,128]{1,0:T(8,128)S(1)} %fusion.12), channel_id=1, source_target_pairs={{0,128},{16,144},{32,160},{48,176},{64,192},{80,208},{96,224},{112... | collective-permute-start | bytes 393224 | tf_op jit(solution)/shard_map/ppermute | solution.py:13
  59.2 3.8 %collective-permute-start.9 = (f32[256,128]{1,0:T(8,128)S(1)}, f32[256,128]{1,0:T(8,128)S(1)}, u32[]{:S(2)}, u32[]{:S(2)}) collective-permute-start(f32[256,128]{1,0:T(8,128)S(1)} %fusion.11), channel_id=1, source_target_pairs={{0,128},{16,144},{32,160},{48,176},{64,192},{80,208},{96,224},{112... | collective-permute-start | bytes 393224 | tf_op jit(solution)/shard_map/ppermute | solution.py:13
  63.6 6.0 %collective-permute-start.10 = (f32[256,128]{1,0:T(8,128)S(1)}, f32[256,128]{1,0:T(8,128)S(1)}, u32[]{:S(2)}, u32[]{:S(2)}) collective-permute-start(f32[256,128]{1,0:T(8,128)S(1)} %fusion.10), channel_id=1, source_target_pairs={{0,128},{16,144},{32,160},{48,176},{64,192},{80,208},{96,224},{112... | collective-permute-start | bytes 393224 | tf_op jit(solution)/shard_map/ppermute | solution.py:13
  69.8 0.3 fusion.9
  70.1 3.8 %collective-permute-start.11 = (f32[256,128]{1,0:T(8,128)S(1)}, f32[256,128]{1,0:T(8,128)S(1)}, u32[]{:S(2)}, u32[]{:S(2)}) collective-permute-start(f32[256,128]{1,0:T(8,128)S(1)} %fusion.9), channel_id=1, source_target_pairs={{0,128},{16,144},{32,160},{48,176},{64,192},{80,208},{96,224},{112... | collective-permute-start | bytes 393224 | tf_op jit(solution)/shard_map/ppermute | solution.py:13
  74.5 1.9 %collective-permute-start.12 = (f32[256,128]{1,0:T(8,128)S(1)}, f32[256,128]{1,0:T(8,128)S(1)}, u32[]{:S(2)}, u32[]{:S(2)}) collective-permute-start(f32[256,128]{1,0:T(8,128)S(1)} %fusion.8), channel_id=1, source_target_pairs={{0,4},{1,5},{2,6},{3,7},{4,0},{5,1},{6,2},{7,3},{8,12},{9,13},{10,... | collective-permute-start | bytes 393224 | tf_op jit(solution)/shard_map/ppermute | solution.py:13
  77.0 3.9 %collective-permute-start.13 = (f32[256,128]{1,0:T(8,128)S(1)}, f32[256,128]{1,0:T(8,128)S(1)}, u32[]{:S(2)}, u32[]{:S(2)}) collective-permute-start(f32[256,128]{1,0:T(8,128)S(1)} %fusion.7), channel_id=1, source_target_pairs={{0,4},{1,5},{2,6},{3,7},{4,0},{5,1},{6,2},{7,3},{8,12},{9,13},{10,... | collective-permute-start | bytes 393224 | tf_op jit(solution)/shard_map/ppermute | solution.py:13
  81.5 1.9 %collective-permute-start.14 = (f32[256,128]{1,0:T(8,128)S(1)}, f32[256,128]{1,0:T(8,128)S(1)}, u32[]{:S(2)}, u32[]{:S(2)}) collective-permute-start(f32[256,128]{1,0:T(8,128)S(1)} %fusion.6), channel_id=1, source_target_pairs={{0,4},{1,5},{2,6},{3,7},{4,0},{5,1},{6,2},{7,3},{8,12},{9,13},{10,... | collective-permute-start | bytes 393224 | tf_op jit(solution)/shard_map/ppermute | solution.py:13
  83.8 1.5 %collective-permute-done.11 = f32[256,128]{1,0:T(8,128)S(1)} collective-permute-done((f32[256,128]{1,0:T(8,128)S(1)}, f32[256,128]{1,0:T(8,128)S(1)}, u32[]{:S(2)}, u32[]{:S(2)}) %collective-permute-start.11) | collective-permute-done | bytes 131104 | tf_op jit(solution)/shard_map/ppermute | solution.py:13
  85.6 2.4 %collective-permute-start.15 = (f32[256,128]{1,0:T(8,128)S(1)}, f32[256,128]{1,0:T(8,128)S(1)}, u32[]{:S(2)}, u32[]{:S(2)}) collective-permute-start(f32[256,128]{1,0:T(8,128)S(1)} %fusion.5), channel_id=1, source_target_pairs={{0,4},{1,5},{2,6},{3,7},{4,0},{5,1},{6,2},{7,3},{8,12},{9,13},{10,... | collective-permute-start | bytes 393224 | tf_op jit(solution)/shard_map/ppermute | solution.py:13
  88.3 0.3 fusion.4
  88.6 0.4 convolution_bitcast_fusion.4
  89.0 0.3 fusion.3
  89.3 0.4 convolution_bitcast_fusion.3
  90.0 0.4 convolution_bitcast_fusion.2
  90.4 1.1 %maximum_bitcast_fusion = f32[1,1,512,512]{3,2,1,0:T(8,128)} fusion(f32[512,128]{1,0:T(8,128)S(1)} %convolution_bitcast_fusion.2, f32[512,128]{1,0:T(8,128)S(1)} %convolution_bitcast_fusion.3, f32[512,128]{1,0:T(8,128)S(1)} %convolution_bitcast_fusion.4, f32[512]{0:T(512)S(1)} %pad.3.clone), kind=kLoop, calls=%fused_computation.50 | loop fusion | flops 786432 | bytes 1837056 | tf_op jit(solution)/shard_map/broadcast_in_dim | solution.py:61
  91.5 1.0 %collective-permute-done.15 = f32[256,128]{1,0:T(8,128)S(1)} collective-permute-done((f32[256,128]{1,0:T(8,128)S(1)}, f32[256,128]{1,0:T(8,128)S(1)}, u32[]{:S(2)}, u32[]{:S(2)}) %collective-permute-start.15) | collective-permute-done | bytes 131104 | tf_op jit(solution)/shard_map/ppermute | solution.py:13
  92.7 1.1 %fusion = f32[1,1,512,512]{3,2,1,0:T(8,128)} fusion(f32[1,1,512,512]{3,2,1,0:T(8,128)} %maximum_bitcast_fusion, f32[256,128]{1,0:T(8,128)S(1)} %fusion.1, f32[1,1,512,256]{3,2,1,0:T(8,128)S(1)} %copy-done.1), kind=kOutput, calls=%fused_computation.2 | convolution fusion | flops 100663296 | bytes 917504 | tf_op jit(solution)/shard_map/dot_general | solution.py:17
  (46 shorter events, 7.3 us)
Async XLA Ops:
  0.0 1.2 %copy-start = (f32[1,1,512,512]{3,2,1,0:T(8,128)S(1)}, f32[1,1,512,512]{3,2,1,0:T(8,128)}, u32[]{:S(2)}) copy-start(f32[1,1,512,512]{3,2,1,0:T(8,128)} %param.4) | copy-start | bytes 3145732
  0.0 25.6 %copy-start.2 = (f32[1,1,4,256,512]{4,3,2,1,0:T(8,128)S(1)}, f32[1,1,4,256,512]{4,3,2,1,0:T(8,128)}, u32[]{:S(2)}) copy-start(f32[1,1,4,256,512]{4,3,2,1,0:T(8,128)} %param.6) | copy-start | bytes 6291460
  2.9 23.3 %collective-permute-start = (f32[256,128]{1,0:T(8,128)S(1)}, f32[256,128]{1,0:T(8,128)S(1)}, u32[]{:S(2)}, u32[]{:S(2)}) collective-permute-start(f32[256,128]{1,0:T(8,128)S(1)} %get-tuple-element.44), channel_id=1, source_target_pairs={{0,256},{16,272},{32,288},{48,304},{64,320},{80,336},{96,352},{112... | collective-permute-start | bytes 393224 | tf_op jit(solution)/shard_map/ppermute | solution.py:13
  13.9 17.3 %collective-permute-start.1 = (f32[256,128]{1,0:T(8,128)S(1)}, f32[256,128]{1,0:T(8,128)S(1)}, u32[]{:S(2)}, u32[]{:S(2)}) collective-permute-start(f32[256,128]{1,0:T(8,128)S(1)} %get-tuple-element.43), channel_id=1, source_target_pairs={{0,256},{16,272},{32,288},{48,304},{64,320},{80,336},{96,352},{112... | collective-permute-start | bytes 393224 | tf_op jit(solution)/shard_map/ppermute | solution.py:13
  15.8 21.0 %collective-permute-start.2 = (f32[256,128]{1,0:T(8,128)S(1)}, f32[256,128]{1,0:T(8,128)S(1)}, u32[]{:S(2)}, u32[]{:S(2)}) collective-permute-start(f32[256,128]{1,0:T(8,128)S(1)} %get-tuple-element.42), channel_id=1, source_target_pairs={{0,256},{16,272},{32,288},{48,304},{64,320},{80,336},{96,352},{112... | collective-permute-start | bytes 393224 | tf_op jit(solution)/shard_map/ppermute | solution.py:13
  23.6 18.6 %collective-permute-start.3 = (f32[256,128]{1,0:T(8,128)S(1)}, f32[256,128]{1,0:T(8,128)S(1)}, u32[]{:S(2)}, u32[]{:S(2)}) collective-permute-start(f32[256,128]{1,0:T(8,128)S(1)} %get-tuple-element.41), channel_id=1, source_target_pairs={{0,256},{16,272},{32,288},{48,304},{64,320},{80,336},{96,352},{112... | collective-permute-start | bytes 393224 | tf_op jit(solution)/shard_map/ppermute | solution.py:13
  26.5 25.8 %collective-permute-start.4 = (f32[256,128]{1,0:T(8,128)S(1)}, f32[256,128]{1,0:T(8,128)S(1)}, u32[]{:S(2)}, u32[]{:S(2)}) collective-permute-start(f32[256,128]{1,0:T(8,128)S(1)} %fusion.16), channel_id=1, source_target_pairs={{0,8},{1,9},{2,10},{3,11},{4,12},{5,13},{6,14},{7,15},{8,0},{9,1},... | collective-permute-start | bytes 393224 | tf_op jit(solution)/shard_map/ppermute | solution.py:13
  31.4 27.5 %collective-permute-start.5 = (f32[256,128]{1,0:T(8,128)S(1)}, f32[256,128]{1,0:T(8,128)S(1)}, u32[]{:S(2)}, u32[]{:S(2)}) collective-permute-start(f32[256,128]{1,0:T(8,128)S(1)} %fusion.15), channel_id=1, source_target_pairs={{0,8},{1,9},{2,10},{3,11},{4,12},{5,13},{6,14},{7,15},{8,0},{9,1},... | collective-permute-start | bytes 393224 | tf_op jit(solution)/shard_map/ppermute | solution.py:13
  37.1 26.2 %collective-permute-start.6 = (f32[256,128]{1,0:T(8,128)S(1)}, f32[256,128]{1,0:T(8,128)S(1)}, u32[]{:S(2)}, u32[]{:S(2)}) collective-permute-start(f32[256,128]{1,0:T(8,128)S(1)} %fusion.14), channel_id=1, source_target_pairs={{0,8},{1,9},{2,10},{3,11},{4,12},{5,13},{6,14},{7,15},{8,0},{9,1},... | collective-permute-start | bytes 393224 | tf_op jit(solution)/shard_map/ppermute | solution.py:13
  42.5 27.3 %collective-permute-start.7 = (f32[256,128]{1,0:T(8,128)S(1)}, f32[256,128]{1,0:T(8,128)S(1)}, u32[]{:S(2)}, u32[]{:S(2)}) collective-permute-start(f32[256,128]{1,0:T(8,128)S(1)} %fusion.13), channel_id=1, source_target_pairs={{0,8},{1,9},{2,10},{3,11},{4,12},{5,13},{6,14},{7,15},{8,0},{9,1},... | collective-permute-start | bytes 393224 | tf_op jit(solution)/shard_map/ppermute | solution.py:13
  52.6 21.6 %collective-permute-start.8 = (f32[256,128]{1,0:T(8,128)S(1)}, f32[256,128]{1,0:T(8,128)S(1)}, u32[]{:S(2)}, u32[]{:S(2)}) collective-permute-start(f32[256,128]{1,0:T(8,128)S(1)} %fusion.12), channel_id=1, source_target_pairs={{0,128},{16,144},{32,160},{48,176},{64,192},{80,208},{96,224},{112... | collective-permute-start | bytes 393224 | tf_op jit(solution)/shard_map/ppermute | solution.py:13
  59.2 17.6 %collective-permute-start.9 = (f32[256,128]{1,0:T(8,128)S(1)}, f32[256,128]{1,0:T(8,128)S(1)}, u32[]{:S(2)}, u32[]{:S(2)}) collective-permute-start(f32[256,128]{1,0:T(8,128)S(1)} %fusion.11), channel_id=1, source_target_pairs={{0,128},{16,144},{32,160},{48,176},{64,192},{80,208},{96,224},{112... | collective-permute-start | bytes 393224 | tf_op jit(solution)/shard_map/ppermute | solution.py:13
  63.6 17.7 %collective-permute-start.10 = (f32[256,128]{1,0:T(8,128)S(1)}, f32[256,128]{1,0:T(8,128)S(1)}, u32[]{:S(2)}, u32[]{:S(2)}) collective-permute-start(f32[256,128]{1,0:T(8,128)S(1)} %fusion.10), channel_id=1, source_target_pairs={{0,128},{16,144},{32,160},{48,176},{64,192},{80,208},{96,224},{112... | collective-permute-start | bytes 393224 | tf_op jit(solution)/shard_map/ppermute | solution.py:13
  70.1 15.2 %collective-permute-start.11 = (f32[256,128]{1,0:T(8,128)S(1)}, f32[256,128]{1,0:T(8,128)S(1)}, u32[]{:S(2)}, u32[]{:S(2)}) collective-permute-start(f32[256,128]{1,0:T(8,128)S(1)} %fusion.9), channel_id=1, source_target_pairs={{0,128},{16,144},{32,160},{48,176},{64,192},{80,208},{96,224},{112... | collective-permute-start | bytes 393224 | tf_op jit(solution)/shard_map/ppermute | solution.py:13
  74.5 13.8 %collective-permute-start.12 = (f32[256,128]{1,0:T(8,128)S(1)}, f32[256,128]{1,0:T(8,128)S(1)}, u32[]{:S(2)}, u32[]{:S(2)}) collective-permute-start(f32[256,128]{1,0:T(8,128)S(1)} %fusion.8), channel_id=1, source_target_pairs={{0,4},{1,5},{2,6},{3,7},{4,0},{5,1},{6,2},{7,3},{8,12},{9,13},{10,... | collective-permute-start | bytes 393224 | tf_op jit(solution)/shard_map/ppermute | solution.py:13
  76.7 11.9 %copy-start.1 = (f32[1,1,512,256]{3,2,1,0:T(8,128)S(1)}, f32[1,1,512,256]{3,2,1,0:T(8,128)}, u32[]{:S(2)}) copy-start(f32[1,1,512,256]{3,2,1,0:T(8,128)} %param.7) | copy-start | bytes 1572868
  77.0 11.9 %collective-permute-start.13 = (f32[256,128]{1,0:T(8,128)S(1)}, f32[256,128]{1,0:T(8,128)S(1)}, u32[]{:S(2)}, u32[]{:S(2)}) collective-permute-start(f32[256,128]{1,0:T(8,128)S(1)} %fusion.7), channel_id=1, source_target_pairs={{0,4},{1,5},{2,6},{3,7},{4,0},{5,1},{6,2},{7,3},{8,12},{9,13},{10,... | collective-permute-start | bytes 393224 | tf_op jit(solution)/shard_map/ppermute | solution.py:13
  81.5 8.1 %collective-permute-start.14 = (f32[256,128]{1,0:T(8,128)S(1)}, f32[256,128]{1,0:T(8,128)S(1)}, u32[]{:S(2)}, u32[]{:S(2)}) collective-permute-start(f32[256,128]{1,0:T(8,128)S(1)} %fusion.6), channel_id=1, source_target_pairs={{0,4},{1,5},{2,6},{3,7},{4,0},{5,1},{6,2},{7,3},{8,12},{9,13},{10,... | collective-permute-start | bytes 393224 | tf_op jit(solution)/shard_map/ppermute | solution.py:13
  85.6 6.9 %collective-permute-start.15 = (f32[256,128]{1,0:T(8,128)S(1)}, f32[256,128]{1,0:T(8,128)S(1)}, u32[]{:S(2)}, u32[]{:S(2)}) collective-permute-start(f32[256,128]{1,0:T(8,128)S(1)} %fusion.5), channel_id=1, source_target_pairs={{0,4},{1,5},{2,6},{3,7},{4,0},{5,1},{6,2},{7,3},{8,12},{9,13},{10,... | collective-permute-start | bytes 393224 | tf_op jit(solution)/shard_map/ppermute | solution.py:13
